TPU v7x, 512 devices: a whole 4x4x16 slice. The times are simulated.
512 devices in a mesh: pages: 128 (over x, z, core), queries: 4 (over y).
Axes of the slice: x: 4, y: 4, z: 16, core: 2. Of those that a mesh axis runs over, the one named last changes fastest.
Arguments:
- query_tokens: bfloat16 [128, 32, 128], P('pages'), may hold values from -1 to 1
- page_patches: bfloat16 [256, 1536, 128], P('pages', 'queries'), may hold values from -1 to 1, as said below
- patch_counts: int32 [256], P('pages'), may hold values from 512 to 1536, as said below
- positive_page: int32 [128], replicated, may hold values from 0 to 255
Outputs:
- query_loss: float32 [128], replicated
- query_grad: float32 [128, 32, 128], P('pages', 'queries')
- page_grad: float32 [256, 1536, 128], P('pages', 'queries')
Inputs may be any that keep to these rules, and one draw needn't show every extreme that they name: `patch_counts`: each page's number of valid patches; some page has exactly 1536. `page_patches`: slots at or past a page's count hold arbitrary values.
All inputs are finite; a program needn't handle non-finite values.
Results may differ from a plain program's by a relative error of at most 0.0028.
Values may be sent and summed in bfloat16 or wider, within the bound.
A program may use at most 64 MiB of HBM per device.

v0:
```python
import jax
import jax.numpy as jnp
from jax import lax
from jax.sharding import PartitionSpec as P

smooth_tau = 0.05
page_temp = 0.02
neg_large = -1e30


def combined_all(part, axis, combine):
    gathered = jax.tree.map(lambda a: lax.all_gather(a, axis), part)

    def take(source):
        return jax.tree.map(lambda a: lax.dynamic_index_in_dim(a, source, 0, False), gathered)

    return lax.fori_loop(
        1, lax.axis_size(axis), lambda source, state: combine(state, take(source)), take(0)
    )


def merge_patch(first, second):
    highest = jnp.maximum(first[0], second[0])
    run_total = first[1] * jnp.exp((first[0] - highest) / smooth_tau) + second[1] * jnp.exp(
        (second[0] - highest) / smooth_tau
    )
    return (highest, run_total)


def merge_page(first, second):
    highest = jnp.maximum(first[0], second[0])
    run_total = first[1] * jnp.exp(first[0] - highest) + second[1] * jnp.exp(second[0] - highest)
    return (highest, run_total, first[2] + second[2])


def shards(query_tokens, page_patches, patch_counts, positive_page):
    group_slot = lax.axis_index("queries")
    gathered = lax.all_gather(query_tokens, "pages", axis=0, tiled=True)
    query_count, query_len, embed_width = gathered.shape
    token_rows = gathered.reshape(query_count * query_len, embed_width)
    row_total = token_rows.shape[0]
    block_rows = min(2048, row_total)
    block_count = row_total // block_rows
    page_local, patch_local, _ = page_patches.shape
    tile_rows = min(128, patch_local)
    live_rows = jnp.clip(patch_counts - group_slot * patch_local, 0, patch_local)
    tile_count = (live_rows + tile_rows - 1) // tile_rows
    tile_pos = jnp.arange(tile_rows, dtype=jnp.int32)

    def tile_scores(block_tokens, page_slab, live_count, tile_idx):
        row_start = tile_idx * tile_rows
        patch_tile = lax.dynamic_slice_in_dim(page_slab, row_start, tile_rows, 0)
        valid_mask = row_start + tile_pos < live_count
        similar = jnp.einsum(
            "re,pe->rp", block_tokens, patch_tile, preferred_element_type=jnp.float32
        )
        return (patch_tile, valid_mask, jnp.where(valid_mask[None, :], similar, neg_large))

    highest_list = []
    total_list = []
    score_list = []
    for page_idx in range(page_local):
        page_slab = page_patches[page_idx]
        live_count = live_rows[page_idx]
        steps_here = tile_count[page_idx]

        def forward_block(block_idx, loop_state):
            highest, run_total, score_page = loop_state
            offset = block_idx * block_rows
            block_tokens = lax.dynamic_slice_in_dim(token_rows, offset, block_rows, 0)

            def forward_tile(tile_idx, inner_state):
                run_max, run_sum, score_buf = inner_state
                _, valid_mask, masked = tile_scores(block_tokens, page_slab, live_count, tile_idx)
                new_max = jnp.maximum(run_max, jnp.max(masked, axis=1))
                fresh_terms = jnp.where(
                    valid_mask[None, :], jnp.exp((masked - new_max[:, None]) / smooth_tau), 0.0
                )
                new_sum = run_sum * jnp.exp((run_max - new_max) / smooth_tau) + jnp.sum(
                    fresh_terms, axis=1
                )
                return (new_max, new_sum, score_buf)

            start_state = (
                jnp.full((block_rows,), neg_large, jnp.float32),
                jnp.zeros((block_rows,), jnp.float32),
                score_page,
            )
            run_max, run_sum, score_page = lax.fori_loop(0, steps_here, forward_tile, start_state)
            highest = lax.dynamic_update_slice_in_dim(highest, run_max, offset, 0)
            run_total = lax.dynamic_update_slice_in_dim(run_total, run_sum, offset, 0)
            return (highest, run_total, score_page)

        score_start = jnp.zeros((1, 1), jnp.float32)
        start_page = (
            jnp.full((row_total,), neg_large, jnp.float32),
            jnp.zeros((row_total,), jnp.float32),
            score_start,
        )
        highest, run_total, score_page = lax.fori_loop(0, block_count, forward_block, start_page)
        highest_list.append(highest)
        total_list.append(run_total)
        score_list.append(score_page)
    highest, run_total = combined_all(
        (jnp.stack(highest_list), jnp.stack(total_list)), "queries", merge_patch
    )
    patch_lse = highest + smooth_tau * jnp.log(run_total)
    smooth = patch_lse - smooth_tau * jnp.log(patch_counts.astype(jnp.float32))[:, None]
    logits = smooth.reshape(page_local, query_count, query_len).sum(axis=2) / page_temp
    page_ids = lax.axis_index("pages") * page_local + jnp.arange(page_local, dtype=jnp.int32)
    is_positive = page_ids[:, None] == positive_page[None, :]
    local_max = jnp.max(logits, axis=0)
    local_sum = jnp.sum(jnp.exp(logits - local_max[None, :]), axis=0)
    local_pos = jnp.sum(jnp.where(is_positive, logits, 0.0), axis=0)
    page_max, page_sum, page_pos = combined_all(
        (local_max, local_sum, local_pos), "pages", merge_page
    )
    query_loss = page_max + jnp.log(page_sum) - page_pos
    weights = (
        jnp.exp(logits - page_max[None, :]) / page_sum[None, :] - is_positive.astype(jnp.float32)
    ) / page_temp
    row_weights = jnp.broadcast_to(
        weights[:, :, None], (page_local, query_count, query_len)
    ).reshape(page_local, row_total)
    grad_rows = jnp.zeros((row_total, embed_width), jnp.float32)
    grad_list = []
    for page_idx in range(page_local):
        page_slab = page_patches[page_idx]
        live_count = live_rows[page_idx]
        steps_here = tile_count[page_idx]
        page_lse = patch_lse[page_idx]
        page_weight = row_weights[page_idx]
        score_page = score_list[page_idx]

        def backward_block(block_idx, loop_state):
            grad_all, grad_slab = loop_state
            offset = block_idx * block_rows
            block_tokens = lax.dynamic_slice_in_dim(token_rows, offset, block_rows, 0)
            block_lse = lax.dynamic_slice_in_dim(page_lse, offset, block_rows, 0)
            block_weight = lax.dynamic_slice_in_dim(page_weight, offset, block_rows, 0)

            def backward_tile(tile_idx, inner_state):
                grad_block, slab_grad = inner_state
                row_start = tile_idx * tile_rows
                patch_tile, valid_mask, masked = tile_scores(
                    block_tokens, page_slab, live_count, tile_idx
                )
                prob_tile = jnp.where(
                    valid_mask[None, :], jnp.exp((masked - block_lse[:, None]) / smooth_tau), 0.0
                )
                coef_tile = (block_weight[:, None] * prob_tile).astype(jnp.bfloat16)
                grad_block = grad_block + jnp.dot(
                    coef_tile, patch_tile, preferred_element_type=jnp.float32
                )
                tile_grad = jnp.einsum(
                    "rp,re->pe", coef_tile, block_tokens, preferred_element_type=jnp.float32
                )
                current = lax.dynamic_slice_in_dim(slab_grad, row_start, tile_rows, 0)
                slab_grad = lax.dynamic_update_slice_in_dim(
                    slab_grad, current + tile_grad, row_start, 0
                )
                return (grad_block, slab_grad)

            grad_block = lax.dynamic_slice_in_dim(grad_all, offset, block_rows, 0)
            grad_block, grad_slab = lax.fori_loop(
                0, steps_here, backward_tile, (grad_block, grad_slab)
            )
            grad_all = lax.dynamic_update_slice_in_dim(grad_all, grad_block, offset, 0)
            return (grad_all, grad_slab)

        start_slab = jnp.zeros((patch_local, embed_width), jnp.float32)
        grad_rows, grad_slab = lax.fori_loop(
            0, block_count, backward_block, (grad_rows, start_slab)
        )
        grad_list.append(grad_slab)
    grad_work = jnp.stack(grad_list)
    grad_three = grad_rows.reshape(query_count, query_len, embed_width)
    partial_value = lax.psum_scatter(grad_three, "pages", scatter_dimension=0, tiled=True)
    query_grad = lax.psum_scatter(partial_value, "queries", scatter_dimension=1, tiled=True)
    return (query_loss, query_grad, grad_work)


def solution(mesh):
    in_specs = (P("pages", None, None), P("pages", "queries", None), P("pages"), P())
    out_specs = (P(), P("pages", "queries", None), P("pages", "queries", None))
    return jax.shard_map(shards, mesh=mesh, in_specs=in_specs, out_specs=out_specs, check_vma=False)
```

profile of v0, /device:TPU:2, one launch (start us, length us, event | category | flops | bytes accessed | tf_op | source)
XLA Modules:
  0.0 752.8 jit_solution(8003784564789250477)
XLA Ops:
  10.9 135.5 %all-gather.12.cloned.1.call-done = bf16[128,32,128]{2,1,0:T(8,128)(2,1)} async-done(((bf16[1,32,128]{2,1,0:T(8,128)(2,1)}), bf16[128,32,128]{2,1,0:T(8,128)(2,1)}) %all-gather.12.cloned.1.call-update) | async-done | bytes 1048592 | tf_op jit(solution)/shard_map/all_gather | solution.py:38
  146.5 16.4 %while.217 = (s32[]{:T(128)}, f32[4096]{0:T(1024)S(1)}, f32[4096]{0:T(1024)S(1)}, bf16[4096,128]{1,0:T(8,128)(2,1)}, s32[]{:T(128)}, /*index=5*/s32[]{:T(128)}, ...) while((s32[]{:T(128)}, f32[4096]{0:T(1024)S(1)}, ...), condition=%wide.region_11.12_spmd.clone, body=%wide.region_6.11_spmd.clone.sunk | while | flops 68688144 | bytes 3860742 | solution.py:100
  147.6 6.5 while.223
  154.7 1.1 constant_dynamic-slice_fusion.17
  155.8 6.5 while.223
  162.9 15.9 %while.215 = (s32[]{:T(128)}, f32[4096]{0:T(1024)S(1)}, f32[4096]{0:T(1024)S(1)}, bf16[4096,128]{1,0:T(8,128)(2,1)}, s32[]{:T(128)}, /*index=5*/s32[]{:T(128)}, ...) while((s32[]{:T(128)}, f32[4096]{0:T(1024)S(1)}, ...), condition=%wide.region_5.6_spmd.clone, body=%wide.region_0.5_spmd.clone.sunk | while | flops 68688144 | bytes 3860742 | solution.py:100
  162.9 1.1 constant_dynamic-slice_fusion.16
  164.1 6.2 while.222
  170.9 1.1 constant_dynamic-slice_fusion.16
  172.0 6.2 while.222
  178.8 12.0 %all-gather.5 = f32[4,2,4096]{2,1,0:T(2,128)S(1)} all-gather(f32[1,2,4096]{2,1,0:T(2,128)S(1)} %maximum_bitcast_fusion), channel_id=2, replica_groups=mesh['pages'=128,'queries'=4] {'queries'}, dimensions={0}, use_global_device_ids=true | all-gather | bytes 163840 | tf_op jit(solution)/shard_map/all_gather | solution.py:12
  190.9 12.0 %all-gather.6 = f32[4,2,4096]{2,1,0:T(2,128)S(1)} all-gather(f32[1,2,4096]{2,1,0:T(2,128)S(1)} %maximum_bitcast_fusion.1), channel_id=3, replica_groups=mesh['pages'=128,'queries'=4] {'queries'}, dimensions={0}, use_global_device_ids=true | all-gather | bytes 163840 | tf_op jit(solution)/shard_map/all_gather | solution.py:12
  203.6 73.3 %all-gather.7 = f32[128,1,128]{2,1,0:T(1,128)S(1)} all-gather(f32[1,1,128]{2,1,0:T(1,128)S(1)} %bitcast.124), channel_id=4, replica_groups=mesh['pages'=128,'queries'=4] {'pages'}, dimensions={0}, use_global_device_ids=true | all-gather | bytes 66048 | tf_op jit(solution)/shard_map/all_gather | solution.py:12
  276.9 72.8 %all-gather.8 = f32[128,1,128]{2,1,0:T(1,128)S(1)} all-gather(f32[1,1,128]{2,1,0:T(1,128)S(1)} %bitcast.127), channel_id=5, replica_groups=mesh['pages'=128,'queries'=4] {'pages'}, dimensions={0}, use_global_device_ids=true | all-gather | bytes 66048 | tf_op jit(solution)/shard_map/all_gather | solution.py:12
  349.7 72.7 %all-gather.9 = f32[128,1,128]{2,1,0:T(1,128)S(1)} all-gather(f32[1,1,128]{2,1,0:T(1,128)S(1)} %bitcast.126), channel_id=6, replica_groups=mesh['pages'=128,'queries'=4] {'pages'}, dimensions={0}, use_global_device_ids=true | all-gather | bytes 66048 | tf_op jit(solution)/shard_map/all_gather | solution.py:12
  422.5 6.1 while.213
  428.8 1.5 broadcast_in_dim.108
  430.3 20.6 %while.219 = (s32[]{:T(128)}, f32[4096,128]{1,0:T(8,128)}, f32[384,128]{1,0:T(8,128)S(1)}, bf16[4096,128]{1,0:T(8,128)(2,1)S(1)}, f32[4096]{0:T(1024)S(1)}, /*in...) while((s32[]{:T(128)}, f32[4096,128]{1,0:T(8,128)}, ...), condition=%wide.region_23.24_spmd.clone, body=%wide.region_20.23_spmd.clone.sunk | while | flops 203178240 | bytes 10209454 | solution.py:172
  430.3 1.3 constant_dynamic-slice_fusion.18
  431.7 7.8 %while.224 = (s32[]{:T(128)}, f32[2048,128]{1,0:T(8,128)S(1)}, f32[384,128]{1,0:T(8,128)S(1)}, s32[]{:T(128)}, f32[2048]{0:T(1024)S(1)}, /*index=5*/s32[128]{0:T...) while((s32[]{:T(128)}, f32[2048,128]{1,0:T(8,128)S(1)}, ...), condition=%wide.region_22.22_spmd, body=%wide.region_21.21_spmd.sunk | while | flops 203178240 | bytes 4932943 | solution.py:165
  440.6 1.3 constant_dynamic-slice_fusion.18
  442.0 7.8 %while.224 = (s32[]{:T(128)}, f32[2048,128]{1,0:T(8,128)S(1)}, f32[384,128]{1,0:T(8,128)S(1)}, s32[]{:T(128)}, f32[2048]{0:T(1024)S(1)}, /*index=5*/s32[128]{0:T...) while((s32[]{:T(128)}, f32[2048,128]{1,0:T(8,128)S(1)}, ...), condition=%wide.region_22.22_spmd, body=%wide.region_21.21_spmd.sunk | while | flops 203178240 | bytes 4932943 | solution.py:165
  449.8 1.1 constant_dynamic-update-slice_fusion.4
  451.1 21.1 %while.221 = (s32[]{:T(128)}, f32[4096,128]{1,0:T(8,128)}, f32[384,128]{1,0:T(8,128)S(1)}, bf16[4096,128]{1,0:T(8,128)(2,1)S(1)}, f32[4096]{0:T(1024)S(1)}, /*in...) while((s32[]{:T(128)}, f32[4096,128]{1,0:T(8,128)}, ...), condition=%wide.region_27.28_spmd.clone, body=%wide.region_24.27_spmd.clone.sunk | while | flops 203178240 | bytes 10209454 | solution.py:172
  451.1 1.3 constant_dynamic-slice_fusion.20
  452.5 8.1 %while.225 = (s32[]{:T(128)}, f32[2048,128]{1,0:T(8,128)S(1)}, f32[384,128]{1,0:T(8,128)S(1)}, s32[]{:T(128)}, f32[2048]{0:T(1024)S(1)}, /*index=5*/s32[128]{0:T...) while((s32[]{:T(128)}, f32[2048,128]{1,0:T(8,128)S(1)}, ...), condition=%wide.region_26.26_spmd, body=%wide.region_25.25_spmd.sunk | while | flops 203178240 | bytes 4932943 | solution.py:165
  461.6 1.3 constant_dynamic-slice_fusion.20
  463.0 8.1 %while.225 = (s32[]{:T(128)}, f32[2048,128]{1,0:T(8,128)S(1)}, f32[384,128]{1,0:T(8,128)S(1)}, s32[]{:T(128)}, f32[2048]{0:T(1024)S(1)}, /*index=5*/s32[128]{0:T...) while((s32[]{:T(128)}, f32[2048,128]{1,0:T(8,128)S(1)}, ...), condition=%wide.region_26.26_spmd, body=%wide.region_25.25_spmd.sunk | while | flops 203178240 | bytes 4932943 | solution.py:165
  471.1 1.1 constant_dynamic-update-slice_fusion.5
  472.2 1.3 dynamic-slice
  475.5 252.4 %reduce-scatter.3.cloned.1.call-done = f32[1,32,128]{2,1,0:T(8,128)} async-done(((f32[128,32,128]{2,1,0:T(8,128)}), f32[1,32,128]{2,1,0:T(8,128)}) %reduce-scatter.3.cloned.1.call-update) | async-done | bytes 16400 | tf_op jit(solution)/shard_map/reduce_scatter | solution.py:178
  727.9 17.5 %all-reduce = f32[1,32,128]{2,1,0:T(8,128)S(1)} all-reduce(f32[1,32,128]{2,1,0:T(8,128)} %reduce-scatter.3.cloned.1.call-done), channel_id=8, replica_groups=mesh['pages'=128,'queries'=4] {'queries'}, use_global_device_ids=true, to_apply=%region_29.30.clone | all-reduce | flops 4096 | bytes 32768
  (331 shorter events, 50.7 us)
Async XLA Ops:
  7.2 139.3 %all-gather.12.cloned.1.call-start = ((), (), s32[]{:S(2)}) async-start(), calls=%async_computation.1 | async-start | bytes 1056768 | tf_op jit(solution)/shard_map/all_gather | solution.py:38
  7.9 720.0 %reduce-scatter.3.cloned.1.call-start = ((), (), s32[]{:S(2)}) async-start(), calls=%async_computation.2 | async-start | bytes 2113536 | tf_op jit(solution)/shard_map/reduce_scatter | solution.py:178
  178.8 24.7 %copy-start.1 = (s32[128]{0:T(128)S(1)}, s32[128]{0:T(128)}, u32[]{:S(2)}) copy-start(s32[128]{0:T(128)} %param.27) | copy-start | bytes 1540
  202.9 227.4 %copy-start = (bf16[4096,128]{1,0:T(8,128)(2,1)S(1)}, bf16[4096,128]{1,0:T(8,128)(2,1)}, u32[]{:S(2)}) copy-start(bf16[4096,128]{1,0:T(8,128)(2,1)} %get-tuple-element.2438) | copy-start | bytes 3145732
Sparse Core Ops, SparseCore 0:
  10.9 135.4 all-gather.11
  472.4 255.4 reduce-scatter.2
where the time goes:
time: 754 us; the launch traced here: 753 us
  waiting for transfers between devices  389 us (52%)
  blocking collectives  260 us (34%)
  loops' own time  25.9 us (3%)
  other arithmetic  24.1 us (3%)
  local copies, waits for them, and re-layouts  22 us (3%)
  matrix products  16.9 us (2%)
  between operations  14.8 us (2%)
    reduce_scatter x1, waiting for transfers between devices, shards(): lax.psum_scatter(grad_three, 'pages', scatter_dimension=0, tiled=True)  252 us
    all_gather x5, blocking collectives, combined_all(): gathered = jax.tree.map(lambda a: lax.all_gather(a, axis), part)  243 us
    all_gather x1, waiting for transfers between devices, shards(): gathered = lax.all_gather(query_tokens, 'pages', axis=0, tiled=True)  136 us
    unnamed x1, blocking collectives  17.5 us
  transfers between devices with their start and end apart: 2, of which 2 were waited for; matrix products, arithmetic and copies ran while one was open for 1% of the time, Pallas kernels for 0%

commit v1 on v0

--- a/solution.py
+++ b/solution.py
@@ -6,6 +6,14 @@
 smooth_tau = 0.05
 page_temp = 0.02
 neg_large = -1e30
+
+
+def _fill_local_data(vals, axis_k):
+    part_next = lax.axis_size("pages")
+    field_out = lax.all_to_all(
+        jnp.stack(part_next * [vals], axis=0), axis_name="pages", split_axis=0, concat_axis=0
+    )
+    return jnp.concatenate(field_out, axis=axis_k)
 
 
 def combined_all(part, axis, combine):
@@ -35,7 +43,7 @@
 
 def shards(query_tokens, page_patches, patch_counts, positive_page):
     group_slot = lax.axis_index("queries")
-    gathered = lax.all_gather(query_tokens, "pages", axis=0, tiled=True)
+    gathered = _fill_local_data(query_tokens, 0)
     query_count, query_len, embed_width = gathered.shape
     token_rows = gathered.reshape(query_count * query_len, embed_width)
     row_total = token_rows.shape[0]

time: 754 us -> 686 us (0.910)
  the two profiles are of different devices: /device:TPU:2 before, /device:TPU:4 now
where the time goes in v1:
time: 686 us; the launch traced here: 685 us
  waiting for transfers between devices  309 us (45%)
  blocking collectives  259 us (38%)
  loops' own time  24 us (3%)
  other arithmetic  23.5 us (3%)
  starting transfers between devices  19.8 us (3%)
  local copies, waits for them, and re-layouts  18.8 us (3%)
  matrix products  17 us (2%)
  between operations  14.8 us (2%)
    reduce_scatter x1, waiting for transfers between devices, shards(): lax.psum_scatter(grad_three, 'pages', scatter_dimension=0, tiled=True)  254 us
    all_gather x5, blocking collectives, combined_all(): gathered = jax.tree.map(lambda a: lax.all_gather(a, axis), part)  241 us
    all_to_all x1, waiting for transfers between devices, _fill_local_data(): lax.all_to_all(jnp.stack(part_next * [vals], axis=0), axis_name='pages',...  54.6 us
    all_to_all x1, starting transfers between devices, _fill_local_data(): lax.all_to_all(jnp.stack(part_next * [vals], axis=0), axis_name='pages',...  19.7 us
    unnamed x1, blocking collectives  17.5 us
    lt x24, other arithmetic, tile_scores(): valid_mask = row_start + tile_pos < live_count  14.8 us
  transfers between devices with their start and end apart: 2, of which 2 were waited for; matrix products, arithmetic and copies ran while one was open for 0% of the time, Pallas kernels for 0%

profile of v1, /device:TPU:4, one launch (start us, length us, event | category | flops | bytes accessed | tf_op | source)
XLA Modules:
  0.0 685.5 jit_solution(2993079939851853722)
XLA Ops:
  7.2 1.9 stack.20
  9.0 19.7 %all-to-all-start = ((bf16[128,1,32,128]{3,2,1,0:T(8,128)(2,1)}), bf16[128,1,32,128]{3,2,1,0:T(8,128)(2,1)S(1)}, u32[]{:S(2)}, u32[]{:S(2)}) async-start(bf16[128,1,32,128]{3,2,1,0:T(8,128)(2,1)} %stack.20), calls=%async_computation | async-start | bytes 2097152 | tf_op jit(solution)/shard_map/all_to_all | solution.py:13
  29.5 54.6 %all-to-all-done = bf16[128,1,32,128]{3,2,1,0:T(8,128)(2,1)S(1)} async-done(((bf16[128,1,32,128]{3,2,1,0:T(8,128)(2,1)}), bf16[128,1,32,128]{3,2,1,0:T(8,128)(2,1)S(1)}, u32[]{:S(2)}, u32[]{:S(2)}) %all-to-all-start) | async-done | bytes 1048608 | tf_op jit(solution)/shard_map/all_to_all | solution.py:13
  84.2 13.7 %while.217 = (s32[]{:T(128)}, f32[4096]{0:T(1024)S(1)}, f32[4096]{0:T(1024)S(1)}, bf16[4096,128]{1,0:T(8,128)(2,1)S(1)}, s32[]{:T(128)}, /*index=5*/s32[]{:T(128...) while((s32[]{:T(128)}, f32[4096]{0:T(1024)S(1)}, ...), condition=%wide.region_11.12_spmd.clone, body=%wide.region_6.11_spmd.clone.sunk | while | flops 68688144 | bytes 3860742 | solution.py:108
  84.2 6.2 while.223
  91.1 6.2 while.223
  97.9 13.9 %while.215 = (s32[]{:T(128)}, f32[4096]{0:T(1024)S(1)}, f32[4096]{0:T(1024)S(1)}, bf16[4096,128]{1,0:T(8,128)(2,1)S(1)}, s32[]{:T(128)}, /*index=5*/s32[]{:T(128...) while((s32[]{:T(128)}, f32[4096]{0:T(1024)S(1)}, ...), condition=%wide.region_5.6_spmd.clone, body=%wide.region_0.5_spmd.clone.sunk | while | flops 68688144 | bytes 3860742 | solution.py:108
  98.0 6.2 while.222
  105.0 6.2 while.222
  111.8 12.5 %all-gather.5 = f32[4,2,4096]{2,1,0:T(2,128)S(1)} all-gather(f32[1,2,4096]{2,1,0:T(2,128)S(1)} %maximum_bitcast_fusion), channel_id=2, replica_groups=mesh['pages'=128,'queries'=4] {'queries'}, dimensions={0}, use_global_device_ids=true | all-gather | bytes 163840 | tf_op jit(solution)/shard_map/all_gather | solution.py:20
  124.4 12.0 %all-gather.6 = f32[4,2,4096]{2,1,0:T(2,128)S(1)} all-gather(f32[1,2,4096]{2,1,0:T(2,128)S(1)} %maximum_bitcast_fusion.1), channel_id=3, replica_groups=mesh['pages'=128,'queries'=4] {'queries'}, dimensions={0}, use_global_device_ids=true | all-gather | bytes 163840 | tf_op jit(solution)/shard_map/all_gather | solution.py:20
  137.1 71.7 %all-gather.7 = f32[128,1,128]{2,1,0:T(1,128)S(1)} all-gather(f32[1,1,128]{2,1,0:T(1,128)S(1)} %bitcast.126), channel_id=4, replica_groups=mesh['pages'=128,'queries'=4] {'pages'}, dimensions={0}, use_global_device_ids=true | all-gather | bytes 66048 | tf_op jit(solution)/shard_map/all_gather | solution.py:20
  208.8 72.6 %all-gather.8 = f32[128,1,128]{2,1,0:T(1,128)S(1)} all-gather(f32[1,1,128]{2,1,0:T(1,128)S(1)} %bitcast.129), channel_id=5, replica_groups=mesh['pages'=128,'queries'=4] {'pages'}, dimensions={0}, use_global_device_ids=true | all-gather | bytes 66048 | tf_op jit(solution)/shard_map/all_gather | solution.py:20
  281.4 72.3 %all-gather.9 = f32[128,1,128]{2,1,0:T(1,128)S(1)} all-gather(f32[1,1,128]{2,1,0:T(1,128)S(1)} %bitcast.128), channel_id=6, replica_groups=mesh['pages'=128,'queries'=4] {'pages'}, dimensions={0}, use_global_device_ids=true | all-gather | bytes 66048 | tf_op jit(solution)/shard_map/all_gather | solution.py:20
  353.7 6.0 while.213
  360.0 1.5 broadcast_in_dim.108
  361.5 20.7 %while.219 = (s32[]{:T(128)}, f32[4096,128]{1,0:T(8,128)}, f32[384,128]{1,0:T(8,128)S(1)}, bf16[4096,128]{1,0:T(8,128)(2,1)S(1)}, f32[4096]{0:T(1024)S(1)}, /*in...) while((s32[]{:T(128)}, f32[4096,128]{1,0:T(8,128)}, ...), condition=%wide.region_23.24_spmd.clone, body=%wide.region_20.23_spmd.clone.sunk | while | flops 203178240 | bytes 10209454 | solution.py:180
  361.5 1.3 constant_dynamic-slice_fusion.18
  362.9 7.9 %while.224 = (s32[]{:T(128)}, f32[2048,128]{1,0:T(8,128)S(1)}, f32[384,128]{1,0:T(8,128)S(1)}, s32[]{:T(128)}, f32[2048]{0:T(1024)S(1)}, /*index=5*/s32[128]{0:T...) while((s32[]{:T(128)}, f32[2048,128]{1,0:T(8,128)S(1)}, ...), condition=%wide.region_22.22_spmd, body=%wide.region_21.21_spmd.sunk | while | flops 203178240 | bytes 4932943 | solution.py:173
  370.8 1.1 constant_dynamic-update-slice_fusion.4
  371.8 1.3 constant_dynamic-slice_fusion.18
  373.2 7.8 %while.224 = (s32[]{:T(128)}, f32[2048,128]{1,0:T(8,128)S(1)}, f32[384,128]{1,0:T(8,128)S(1)}, s32[]{:T(128)}, f32[2048]{0:T(1024)S(1)}, /*index=5*/s32[128]{0:T...) while((s32[]{:T(128)}, f32[2048,128]{1,0:T(8,128)S(1)}, ...), condition=%wide.region_22.22_spmd, body=%wide.region_21.21_spmd.sunk | while | flops 203178240 | bytes 4932943 | solution.py:173
  381.1 1.1 constant_dynamic-update-slice_fusion.4
  382.4 20.5 %while.221 = (s32[]{:T(128)}, f32[4096,128]{1,0:T(8,128)}, f32[384,128]{1,0:T(8,128)S(1)}, bf16[4096,128]{1,0:T(8,128)(2,1)S(1)}, f32[4096]{0:T(1024)S(1)}, /*in...) while((s32[]{:T(128)}, f32[4096,128]{1,0:T(8,128)}, ...), condition=%wide.region_27.28_spmd.clone, body=%wide.region_24.27_spmd.clone.sunk | while | flops 203178240 | bytes 10209454 | solution.py:180
  382.4 1.3 constant_dynamic-slice_fusion.20
  383.8 7.8 %while.225 = (s32[]{:T(128)}, f32[2048,128]{1,0:T(8,128)S(1)}, f32[384,128]{1,0:T(8,128)S(1)}, s32[]{:T(128)}, f32[2048]{0:T(1024)S(1)}, /*index=5*/s32[128]{0:T...) while((s32[]{:T(128)}, f32[2048,128]{1,0:T(8,128)S(1)}, ...), condition=%wide.region_26.26_spmd, body=%wide.region_25.25_spmd.sunk | while | flops 203178240 | bytes 4932943 | solution.py:173
  392.6 1.3 constant_dynamic-slice_fusion.20
  394.0 7.8 %while.225 = (s32[]{:T(128)}, f32[2048,128]{1,0:T(8,128)S(1)}, f32[384,128]{1,0:T(8,128)S(1)}, s32[]{:T(128)}, f32[2048]{0:T(1024)S(1)}, /*index=5*/s32[128]{0:T...) while((s32[]{:T(128)}, f32[2048,128]{1,0:T(8,128)S(1)}, ...), condition=%wide.region_26.26_spmd, body=%wide.region_25.25_spmd.sunk | while | flops 203178240 | bytes 4932943 | solution.py:173
  401.8 1.1 constant_dynamic-update-slice_fusion.5
  402.9 1.3 dynamic-slice
  406.1 254.4 %reduce-scatter.3.cloned.1.call-done = f32[1,32,128]{2,1,0:T(8,128)} async-done(((f32[128,32,128]{2,1,0:T(8,128)}), f32[1,32,128]{2,1,0:T(8,128)}) %reduce-scatter.3.cloned.1.call-update) | async-done | bytes 16400 | tf_op jit(solution)/shard_map/reduce_scatter | solution.py:186
  660.5 17.5 %all-reduce = f32[1,32,128]{2,1,0:T(8,128)S(1)} all-reduce(f32[1,32,128]{2,1,0:T(8,128)} %reduce-scatter.3.cloned.1.call-done), channel_id=8, replica_groups=mesh['pages'=128,'queries'=4] {'queries'}, use_global_device_ids=true, to_apply=%region_29.30.clone | all-reduce | flops 4096 | bytes 32768
  (333 shorter events, 46.5 us)
Async XLA Ops:
  7.2 21.7 %copy-start.2 = (s32[2]{0:T(128)S(1)}, s32[2]{0:T(128)}, u32[]{:S(2)}) copy-start(s32[2]{0:T(128)} %param.26) | copy-start | bytes 28
  7.2 22.3 %copy-start = (bf16[2,384,128]{2,1,0:T(8,128)(2,1)S(1)}, bf16[2,384,128]{2,1,0:T(8,128)(2,1)}, u32[]{:S(2)}) copy-start(bf16[2,384,128]{2,1,0:T(8,128)(2,1)} %param.25) | copy-start | bytes 589828
  9.0 75.1 %all-to-all-start = ((bf16[128,1,32,128]{3,2,1,0:T(8,128)(2,1)}), bf16[128,1,32,128]{3,2,1,0:T(8,128)(2,1)S(1)}, u32[]{:S(2)}, u32[]{:S(2)}) async-start(bf16[128,1,32,128]{3,2,1,0:T(8,128)(2,1)} %stack.20), calls=%async_computation | async-start | bytes 2097152 | tf_op jit(solution)/shard_map/all_to_all | solution.py:13
  28.8 631.8 %reduce-scatter.3.cloned.1.call-start = ((), (), s32[]{:S(2)}) async-start(), calls=%async_computation.2 | async-start | bytes 2113536 | tf_op jit(solution)/shard_map/reduce_scatter | solution.py:186
  111.8 25.2 %copy-start.1 = (s32[128]{0:T(128)S(1)}, s32[128]{0:T(128)}, u32[]{:S(2)}) copy-start(s32[128]{0:T(128)} %param.27) | copy-start | bytes 1540
Sparse Core Ops, SparseCore 0:
  403.0 257.4 reduce-scatter.2
